TPU v7x, 32 devices: a whole 2x2x4 slice. The times are simulated.
32 devices in a mesh: fsdp: 4 (over z), replica: 2 (over x), tensor: 4 (over y, core).
Axes of the slice: x: 2, y: 2, z: 4, core: 2. Of those that a mesh axis runs over, the one named last changes fastest.
Arguments:
- tokens: bfloat16 [1024, 8192], P(('fsdp', 'replica')), may hold values from -6 to 6
- weight_codes: bfloat16 [8192, 14336], P('fsdp', 'tensor'), may hold values from -127 to 127, as said below
- scales: float32 [64, 14336], P('fsdp', 'tensor'), may hold values from 3e-05 to 0.0003
- cotangent: bfloat16 [1024, 14336], P(('fsdp', 'replica'), 'tensor'), may hold values from -6 to 6
- sign_bits: int32 [14336], P('tensor'), may hold values from 0 to 1
Outputs:
- activation: bfloat16 [1024, 14336], P(('fsdp', 'replica'), 'tensor')
- input_grad: bfloat16 [1024, 8192], P(('fsdp', 'replica'), 'tensor')
- grad_codes: float32 [8192, 14336], P(('fsdp', 'replica'), 'tensor')
Inputs may be any that keep to these rules, and one draw needn't show every extreme that they name: `weight_codes`: integer values, held exactly.
All inputs are finite; a program needn't handle non-finite values.
Results may differ from a plain program's by a relative error of at most 0.015.
Values may be sent and summed in bfloat16 or wider, within the bound.
A program may use at most 128 MiB of HBM per device.

v0:
```python
import jax
import jax.numpy as jnp
from jax import lax
from jax.sharding import PartitionSpec as P

HB = 128


def hadamard_table(length):
    indices = jnp.arange(length, dtype=jnp.int32)
    intersection_bits = jnp.bitwise_and(indices[:, None], indices[None, :])
    parity = jnp.zeros((length, length), jnp.int32)
    for bit_pos in range(length.bit_length() - 1):
        parity = parity + jnp.bitwise_and(jnp.right_shift(intersection_bits, bit_pos), 1)
    return (1 - 2 * (parity % 2)).astype(jnp.float32)


def rotate_blocks(matrix, sign_bits, scaling):
    height, width = matrix.shape
    signed = matrix * (2 * sign_bits - 1).astype(jnp.float32)[None, :]
    blocks = signed.reshape(height, width // HB, HB)
    turned = jnp.einsum("rbi,ij->rbj", blocks, hadamard_table(HB), precision=lax.Precision.HIGHEST)
    return turned.reshape(height, width) * scaling


def shards(tokens, weight_codes, scales, cotangent, sign_bits):
    local_tokens = tokens.shape[0]
    shard_rows, hidden_cols = weight_codes.shape
    block_rows = shard_rows // scales.shape[0]
    weight = (
        (
            weight_codes.astype(jnp.float32).reshape(scales.shape[0], block_rows, hidden_cols)
            * scales[:, None, :]
        )
        .reshape(shard_rows, hidden_cols)
        .astype(jnp.bfloat16)
    )
    columns = lax.all_to_all(tokens, "fsdp", split_axis=1, concat_axis=0, tiled=True)
    token_rows = columns
    hidden = lax.psum_scatter(
        jnp.dot(token_rows, weight, preferred_element_type=jnp.float32).astype(jnp.bfloat16),
        "fsdp",
        scatter_dimension=0,
        tiled=True,
    ).astype(jnp.float32)
    sigmoid_val = jax.nn.sigmoid(hidden)
    activation = (hidden * sigmoid_val).astype(jnp.bfloat16)
    hidden_grad = (
        cotangent.astype(jnp.float32) * sigmoid_val * (1.0 + hidden * (1.0 - sigmoid_val))
    ).astype(jnp.bfloat16)
    arrived = lax.all_gather(hidden_grad, "fsdp", axis=0, tiled=True)
    token_rows = columns
    weight_grad = lax.dot_general(
        token_rows, arrived, (((0,), (0,)), ((), ())), preferred_element_type=jnp.float32
    )
    product = lax.dot_general(
        arrived, weight, (((1,), (1,)), ((), ())), preferred_element_type=jnp.float32
    ).astype(jnp.bfloat16)
    input_rows = product
    weight_grad, input_rows = (weight_grad, input_rows)
    returned = lax.all_to_all(input_rows, "fsdp", split_axis=0, concat_axis=1, tiled=True)
    input_grad = lax.psum_scatter(
        returned.astype(jnp.float32).astype(jnp.bfloat16), "tensor", scatter_dimension=1, tiled=True
    )
    total_tokens = local_tokens * lax.axis_size("fsdp") * lax.axis_size("replica")
    scaling = 1.0 / jnp.sqrt(jnp.float32(HB) * jnp.float32(total_tokens))
    grad_codes = rotate_blocks(
        lax.psum_scatter(
            weight_grad.astype(jnp.bfloat16), "replica", scatter_dimension=0, tiled=True
        ).astype(jnp.float32),
        sign_bits,
        scaling,
    )
    return (activation, input_grad, grad_codes)


def solution(mesh):
    return jax.shard_map(
        shards,
        mesh=mesh,
        in_specs=(
            P(("fsdp", "replica"), None),
            P("fsdp", "tensor"),
            P("fsdp", "tensor"),
            P(("fsdp", "replica"), "tensor"),
            P("tensor"),
        ),
        out_specs=(
            P(("fsdp", "replica"), "tensor"),
            P(("fsdp", "replica"), "tensor"),
            P(("fsdp", "replica"), "tensor"),
        ),
        check_vma=False,
    )
```

profile of v0, /device:TPU:0, one launch (start us, length us, event | category | flops | bytes accessed | tf_op | source)
XLA Modules:
  0.0 463.2 jit_solution(12384013270102566466)
XLA Ops:
  7.2 0.0 copy-start.1
  7.2 4.1 copy.25
  11.3 6.3 %all-to-all-start = ((bf16[128,4,2048]{0,2,1:T(8,128)(2,1)}), bf16[128,4,2048]{0,2,1:T(8,128)(2,1)S(1)}, u32[]{:S(2)}, u32[]{:S(2)}) async-start(bf16[128,4,2048]{0,2,1:T(8,128)(2,1)} %bitcast.32), calls=%async_computation | async-start | bytes 4194304 | tf_op jit(solution)/shard_map/all_to_all | solution.py:38
  17.6 0.0 reduce-scatter.10.cloned.1.call-start
  17.6 0.0 copy-done.1
  17.6 14.0 %fusion = bf16[2048,3584]{1,0:T(8,128)(2,1)} fusion(bf16[2048,3584]{1,0:T(8,128)(2,1)} %param.6, f32[16,3584]{1,0:T(8,128)S(1)} %copy-done.1), kind=kLoop, calls=%fused_computation.1 | loop fusion | flops 22020096 | bytes 29589504 | tf_op jit(solution)/shard_map/convert_element_type | solution.py:36
  31.7 34.2 %all-to-all-done = bf16[128,4,2048]{0,2,1:T(8,128)(2,1)S(1)} async-done(((bf16[128,4,2048]{0,2,1:T(8,128)(2,1)}), bf16[128,4,2048]{0,2,1:T(8,128)(2,1)S(1)}, u32[]{:S(2)}, u32[]{:S(2)}) %all-to-all-start) | async-done | bytes 2097184 | tf_op jit(solution)/shard_map/all_to_all | solution.py:38
  65.8 2.7 copy.26
  68.5 13.0 %fusion.2 = bf16[512,3584]{0,1:T(8,128)(2,1)} fusion(bf16[2048,3584]{1,0:T(8,128)(2,1)} %fusion, bf16[512,2048]{1,0:T(8,128)(2,1)} %bitcast.34), kind=kOutput, calls=%fused_computation.7 | convolution fusion | flops 7518027776 | bytes 20447232 | tf_op jit(solution)/shard_map/dot_general | solution.py:41
  81.5 6.0 %copy.33 = bf16[512,3584]{1,0:T(8,128)(2,1)} copy(bf16[512,3584]{0,1:T(8,128)(2,1)} %fusion.2) | data formatting | bytes 7340032
  87.5 0.0 reduce-scatter.10.cloned.1.call-update
  87.5 0.0 all-gather.2.cloned.1.call-start
  87.6 1.1 copy-done
  88.7 0.6 copy.27
  89.3 66.1 %reduce-scatter.10.cloned.1.call-done = bf16[128,3584]{1,0:T(8,128)(2,1)} async-done(((bf16[512,3584]{1,0:T(8,128)(2,1)}), bf16[128,3584]{1,0:T(8,128)(2,1)}) %reduce-scatter.10.cloned.1.call-update) | async-done | bytes 917520
  155.4 1.5 copy.34
  156.9 1.8 fusion.9
  158.7 0.0 all-gather.2.cloned.1.call-update
  158.7 0.0 reduce-scatter.8.cloned.1.call-start
  158.8 72.3 %all-gather.2.cloned.1.call-done = bf16[512,3584]{0,1:T(8,128)(2,1)} async-done(((bf16[128,3584]{0,1:T(8,128)(2,1)}), bf16[512,3584]{0,1:T(8,128)(2,1)}) %all-gather.2.cloned.1.call-update) | async-done | bytes 3670032 | tf_op jit(solution)/shard_map/all_gather | solution.py:51
  231.1 13.1 %fusion.1 = bf16[2048,3584]{0,1:T(8,128)(2,1)} fusion(bf16[512,3584]{0,1:T(8,128)(2,1)} %all-gather.2.cloned.1.call-done, bf16[512,2048]{1,0:T(8,128)(2,1)} %bitcast.35), kind=kOutput, calls=%fused_computation.4 | convolution fusion | flops 7523532800 | bytes 20447232 | tf_op jit(solution)/shard_map/dot_general | solution.py:53
  244.2 0.0 reduce-scatter.8.cloned.1.call-update
  244.3 0.2 reduce-scatter.6.cloned.1.call-start
  244.5 12.3 %convolution_convert_fusion.2 = bf16[512,2048]{1,0:T(8,128)(2,1)S(1)} fusion(bf16[512,3584]{0,1:T(8,128)(2,1)} %all-gather.2.cloned.1.call-done, bf16[2048,3584]{1,0:T(8,128)(2,1)} %fusion), kind=kOutput, calls=%fused_computation.8 | convolution fusion | flops 7517241344 | bytes 20447232 | tf_op jit(solution)/shard_map/dot_general | solution.py:56
  256.8 50.6 %all_to_all.38 = bf16[4,128,2048]{2,1,0:T(8,128)(2,1)S(1)} all-to-all(bf16[4,128,2048]{2,1,0:T(8,128)(2,1)S(1)} %bitcast.36), channel_id=1, replica_groups=mesh['fsdp'=4,'replica'=2,'tensor'=4] {'fsdp'}, dimensions={0} | all-to-all | bytes 4194304 | tf_op jit(solution)/shard_map/all_to_all | solution.py:61
  307.5 1.5 copy.35
  308.9 0.0 reduce-scatter.6.cloned.1.call-update
  309.0 1.3 copy.30
  310.3 99.5 %reduce-scatter.8.cloned.1.call-done = bf16[1024,3584]{0,1:T(8,128)(2,1)} async-done(((bf16[2048,3584]{0,1:T(8,128)(2,1)}), bf16[1024,3584]{0,1:T(8,128)(2,1)}) %reduce-scatter.8.cloned.1.call-update) | async-done | bytes 7340048 | tf_op jit(solution)/shard_map/reduce_scatter | solution.py:68
  409.7 9.6 %convert_multiply_fusion = f32[1024,3584]{0,1:T(8,128)} fusion(bf16[1024,3584]{0,1:T(8,128)(2,1)} %reduce-scatter.8.cloned.1.call-done, f32[3584]{0:T(1024)S(1)} %add_convert_fusion), kind=kLoop, calls=%fused_computation.3 | loop fusion | flops 7340032 | bytes 22034432 | tf_op jit(solution)/shard_map/mul | solution.py:20
  419.3 23.1 %convolution_multiply_fusion = f32[1024,28,128]{0,2,1:T(8,128)} fusion(f32[1024,28,128]{0,2,1:T(8,128)} %bitcast.29), kind=kOutput, calls=%fused_computation.5 | convolution fusion | flops 5641388032 | bytes 29360128 | tf_op jit(solution)/shard_map/rbi,ij->rbj/dot_general | solution.py:22
  442.4 14.3 %copy.31 = f32[1024,3584]{1,0:T(8,128)} copy(f32[1024,3584]{0,1:T(8,128)} %bitcast.28) | data formatting | bytes 29360128
  (5 shorter events, 0.0 us)
Async XLA Ops:
  7.2 10.5 %copy-start.1 = (f32[16,3584]{1,0:T(8,128)S(1)}, f32[16,3584]{1,0:T(8,128)}, u32[]{:S(2)}) copy-start(f32[16,3584]{1,0:T(8,128)} %param.7) | copy-start | bytes 688132
  11.3 54.5 %all-to-all-start = ((bf16[128,4,2048]{0,2,1:T(8,128)(2,1)}), bf16[128,4,2048]{0,2,1:T(8,128)(2,1)S(1)}, u32[]{:S(2)}, u32[]{:S(2)}) async-start(bf16[128,4,2048]{0,2,1:T(8,128)(2,1)} %bitcast.32), calls=%async_computation | async-start | bytes 4194304 | tf_op jit(solution)/shard_map/all_to_all | solution.py:38
  17.6 137.7 %reduce-scatter.10.cloned.1.call-start = ((), (), s32[]{:S(2)}) async-start(), calls=%async_computation.8 | async-start | bytes 4587520
  87.5 1.2 copy-start
  87.5 143.6 %all-gather.2.cloned.1.call-start = ((), (), s32[]{:S(2)}) async-start(), calls=%async_computation.5 | async-start | bytes 4587520 | tf_op jit(solution)/shard_map/all_gather | solution.py:51
  158.7 251.0 %reduce-scatter.8.cloned.1.call-start = ((), (), s32[]{:S(2)}) async-start(), calls=%async_computation.7 | async-start | bytes 22020096 | tf_op jit(solution)/shard_map/reduce_scatter | solution.py:68
  244.3 212.4 %reduce-scatter.6.cloned.1.call-start = ((), (), s32[]{:S(2)}) async-start(), calls=%async_computation.6 | async-start | bytes 2621440 | tf_op jit(solution)/shard_map/reduce_scatter | solution.py:62
  307.5 1.5 copy-start.2
Sparse Core Ops, SparseCore 0:
  87.7 67.6 reduce-scatter.9
  158.9 72.1 all-gather.1
  244.4 165.3 reduce-scatter.7
  412.7 31.1 reduce-scatter.5
where the time goes:
time: 464 us; the launch traced here: 463 us
  waiting for transfers between devices  272 us (59%)
  matrix products  61.6 us (13%)
  blocking collectives  50.6 us (11%)
  local copies, waits for them, and re-layouts  33 us (7%)
  other arithmetic  25.4 us (5%)
  between operations  13.8 us (3%)
  starting transfers between devices  6.65 us (1%)
    reduce_scatter x1, waiting for transfers between devices, shards(): lax.psum_scatter(weight_grad.astype(jnp.bfloat16), 'replica', scatter_dim...  99.5 us
    all_gather x1, waiting for transfers between devices, shards(): arrived = lax.all_gather(hidden_grad, 'fsdp', axis=0, tiled=True)  72.3 us
    unnamed x5, waiting for transfers between devices  66.1 us
    all_to_all x1, blocking collectives, shards(): lax.all_to_all(input_rows, 'fsdp', split_axis=0, concat_axis=1, tiled=True)  50.6 us
    all_to_all x1, waiting for transfers between devices, shards(): lax.all_to_all(tokens, 'fsdp', split_axis=1, concat_axis=0, tiled=True)  34.2 us
    unnamed x12, local copies, waits for them, and re-layouts  28.9 us
    dot_general x1, matrix products, rotate_blocks(): jnp.einsum('rbi,ij->rbj', blocks, hadamard_table(HB), precision=lax.Preci...  23.1 us
    convert_element_type x1, other arithmetic, shards(): weight = (weight_codes.astype(jnp.float32).reshape(scales.shape[0], block...  14 us
  transfers between devices with their start and end apart: 5, of which 4 were waited for; matrix products, arithmetic and copies ran while one was open for 17% of the time, Pallas kernels for 0%

commit v1 on v0

--- a/solution.py
+++ b/solution.py
@@ -48,7 +48,12 @@
     hidden_grad = (
         cotangent.astype(jnp.float32) * sigmoid_val * (1.0 + hidden * (1.0 - sigmoid_val))
     ).astype(jnp.bfloat16)
-    arrived = lax.all_gather(hidden_grad, "fsdp", axis=0, tiled=True)
+    ring = [hidden_grad]
+    for hop in range(3):
+        ring.append(lax.ppermute(ring[-1], "fsdp", [(dev, (dev + 1) % 4) for dev in range(4)]))
+    arrived = jnp.roll(
+        jnp.concatenate(ring[::-1], axis=0), (lax.axis_index("fsdp") + 1) * ring[0].shape[0], axis=0
+    )
     token_rows = columns
     weight_grad = lax.dot_general(
         token_rows, arrived, (((0,), (0,)), ((), ())), preferred_element_type=jnp.float32

time: 464 us -> 469 us (1.011)
  local copies, waits for them, and re-layouts: 33 us -> 42.9 us
    all_gather x1 -> x0, waiting for transfers between devices: 72.3 us -> none  [shards(): arrived = lax.all_gather(hidden_grad, 'fsdp', axis=0, tiled=True)]
    ppermute x0 -> x3, waiting for transfers between devices: none -> 67.1 us  [shards(): lax.ppermute(ring[-1], 'fsdp', [(dev, (dev + 1) % 4) for dev in range(4)])]
    unnamed x12 -> x23, local copies, waits for them, and re-layouts: 28.9 us -> 38.4 us
    unnamed x5 -> x4, waiting for transfers between devices: 66.1 us -> 67.2 us
  transfers between devices with their start and end apart: 5 -> 7, of which waited for: 4 -> 6; matrix products, arithmetic and copies ran while one was open for 17% -> 16% of each run, Pallas kernels for 0% -> 0%
where the time goes in v1:
time: 469 us; the launch traced here: 468 us
  waiting for transfers between devices  271 us (58%)
  matrix products  59.5 us (13%)
  blocking collectives  48 us (10%)
  local copies, waits for them, and re-layouts  42.9 us (9%)
  other arithmetic  25.6 us (5%)
  between operations  13.9 us (3%)
  starting transfers between devices  7.74 us (2%)
    reduce_scatter x1, waiting for transfers between devices, shards(): lax.psum_scatter(weight_grad.astype(jnp.bfloat16), 'replica', scatter_dim...  102 us
    unnamed x4, waiting for transfers between devices  67.2 us
    ppermute x3, waiting for transfers between devices, shards(): lax.ppermute(ring[-1], 'fsdp', [(dev, (dev + 1) % 4) for dev in range(4)])  67.1 us
    all_to_all x1, blocking collectives, shards(): lax.all_to_all(input_rows, 'fsdp', split_axis=0, concat_axis=1, tiled=True)  48 us
    unnamed x23, local copies, waits for them, and re-layouts  38.4 us
    all_to_all x1, waiting for transfers between devices, shards(): lax.all_to_all(tokens, 'fsdp', split_axis=1, concat_axis=0, tiled=True)  34.2 us
    dot_general x1, matrix products, rotate_blocks(): jnp.einsum('rbi,ij->rbj', blocks, hadamard_table(HB), precision=lax.Preci...  23.1 us
    convert_element_type x1, other arithmetic, shards(): weight = (weight_codes.astype(jnp.float32).reshape(scales.shape[0], block...  14 us
  transfers between devices with their start and end apart: 7, of which 6 were waited for; matrix products, arithmetic and copies ran while one was open for 16% of the time, Pallas kernels for 0%

profile of v1, /device:TPU:0, one launch (start us, length us, event | category | flops | bytes accessed | tf_op | source)
XLA Modules:
  0.0 468.3 jit_solution(3512316599479265190)
XLA Ops:
  7.2 4.1 copy.25
  11.3 6.3 %all-to-all-start = ((bf16[128,4,2048]{0,2,1:T(8,128)(2,1)}), bf16[128,4,2048]{0,2,1:T(8,128)(2,1)S(1)}, u32[]{:S(2)}, u32[]{:S(2)}) async-start(bf16[128,4,2048]{0,2,1:T(8,128)(2,1)} %bitcast.30), calls=%async_computation | async-start | bytes 4194304 | tf_op jit(solution)/shard_map/all_to_all | solution.py:38
  17.6 14.0 %fusion = bf16[2048,3584]{1,0:T(8,128)(2,1)} fusion(bf16[2048,3584]{1,0:T(8,128)(2,1)} %param.6, f32[16,3584]{1,0:T(8,128)S(1)} %copy-done.2), kind=kLoop, calls=%fused_computation.1 | loop fusion | flops 22020096 | bytes 29589504 | tf_op jit(solution)/shard_map/convert_element_type | solution.py:36
  31.7 34.2 %all-to-all-done = bf16[128,4,2048]{0,2,1:T(8,128)(2,1)S(1)} async-done(((bf16[128,4,2048]{0,2,1:T(8,128)(2,1)}), bf16[128,4,2048]{0,2,1:T(8,128)(2,1)S(1)}, u32[]{:S(2)}, u32[]{:S(2)}) %all-to-all-start) | async-done | bytes 2097184 | tf_op jit(solution)/shard_map/all_to_all | solution.py:38
  65.8 2.7 copy.26
  68.5 13.1 %fusion.2 = bf16[512,3584]{0,1:T(8,128)(2,1)} fusion(bf16[2048,3584]{1,0:T(8,128)(2,1)} %fusion, bf16[512,2048]{1,0:T(8,128)(2,1)} %bitcast.32), kind=kOutput, calls=%fused_computation.7 | convolution fusion | flops 7518027776 | bytes 20447232 | tf_op jit(solution)/shard_map/dot_general | solution.py:41
  81.6 6.1 %copy.33 = bf16[512,3584]{1,0:T(8,128)(2,1)} copy(bf16[512,3584]{0,1:T(8,128)(2,1)} %fusion.2) | data formatting | bytes 7340032
  87.7 0.6 copy.27
  88.4 67.1 %reduce-scatter.10.cloned.1.call-done = bf16[128,3584]{1,0:T(8,128)(2,1)} async-done(((bf16[512,3584]{1,0:T(8,128)(2,1)}), bf16[128,3584]{1,0:T(8,128)(2,1)}) %reduce-scatter.10.cloned.1.call-update) | async-done | bytes 917520
  155.5 2.2 copy.34
  157.7 2.0 fusion.15
  159.7 1.3 collective-permute-start
  161.0 22.3 %collective-permute-done = bf16[128,3584]{0,1:T(8,128)(2,1)S(1)} collective-permute-done((bf16[128,3584]{0,1:T(8,128)(2,1)S(1)}, bf16[128,3584]{0,1:T(8,128)(2,1)S(1)}, u32[]{:S(2)}, u32[]{:S(2)}) %collective-permute-start) | collective-permute-done | bytes 917536 | tf_op jit(solution)/shard_map/ppermute | solution.py:53
  183.3 22.8 %collective-permute-done.1 = bf16[128,3584]{0,1:T(8,128)(2,1)} collective-permute-done((bf16[128,3584]{0,1:T(8,128)(2,1)S(1)}, bf16[128,3584]{0,1:T(8,128)(2,1)}, u32[]{:S(2)}, u32[]{:S(2)}) %collective-permute-start.1) | collective-permute-done | bytes 917536 | tf_op jit(solution)/shard_map/ppermute | solution.py:53
  206.1 22.1 %collective-permute-done.2 = bf16[128,3584]{0,1:T(8,128)(2,1)} collective-permute-done((bf16[128,3584]{0,1:T(8,128)(2,1)}, bf16[128,3584]{0,1:T(8,128)(2,1)}, u32[]{:S(2)}, u32[]{:S(2)}) %collective-permute-start.2) | collective-permute-done | bytes 917536 | tf_op jit(solution)/shard_map/ppermute | solution.py:53
  228.2 1.4 constant_dynamic-update-slice_fusion.7
  229.6 1.5 constant_dynamic-update-slice_fusion.6
  231.1 0.3 constant_dynamic-update-slice_fusion.5
  231.4 0.3 constant_dynamic-update-slice_fusion.4
  231.8 1.5 constant_dynamic-update-slice_fusion.3
  233.3 1.5 constant_dynamic-update-slice_fusion.2
  235.1 0.3 constant_dynamic-update-slice_fusion
  235.4 3.0 copy-done.3
  238.4 11.0 %fusion.1 = bf16[2048,3584]{0,1:T(8,128)(2,1)} fusion(bf16[512,2048]{1,0:T(8,128)(2,1)S(1)} %bitcast.33, bf16[1024,3584]{0,1:T(8,128)(2,1)S(1)} %constant_dynamic-update-slice_fusion, s32[]{:T(128)S(6)} %select_n.20), kind=kOutput, calls=%fused_computation.4 | convolution fusion | flops 7523532800 | bytes 20447236 | tf_op jit(solution)/shard_map/dot_general | solution.py:58
  249.5 12.3 %fusion.6 = bf16[512,2048]{1,0:T(8,128)(2,1)S(1)} fusion(bf16[2048,3584]{1,0:T(8,128)(2,1)} %fusion, bf16[1024,3584]{0,1:T(8,128)(2,1)} %copy-done.3, s32[]{:T(128)S(6)} %select_n.20), kind=kOutput, calls=%fused_computation.11 | convolution fusion | flops 7517241344 | bytes 20447236 | tf_op jit(solution)/shard_map/dot_general | solution.py:61
  261.8 48.0 %all_to_all.38 = bf16[4,128,2048]{2,1,0:T(8,128)(2,1)S(1)} all-to-all(bf16[4,128,2048]{2,1,0:T(8,128)(2,1)S(1)} %bitcast.34), channel_id=1, replica_groups=mesh['fsdp'=4,'replica'=2,'tensor'=4] {'fsdp'}, dimensions={0} | all-to-all | bytes 4194304 | tf_op jit(solution)/shard_map/all_to_all | solution.py:66
  309.8 1.5 copy.35
  311.3 1.3 copy.30
  312.6 102.2 %reduce-scatter.8.cloned.1.call-done = bf16[1024,3584]{0,1:T(8,128)(2,1)} async-done(((bf16[2048,3584]{0,1:T(8,128)(2,1)}), bf16[1024,3584]{0,1:T(8,128)(2,1)}) %reduce-scatter.8.cloned.1.call-update) | async-done | bytes 7340048 | tf_op jit(solution)/shard_map/reduce_scatter | solution.py:73
  414.8 9.6 %convert_multiply_fusion = f32[1024,3584]{0,1:T(8,128)} fusion(bf16[1024,3584]{0,1:T(8,128)(2,1)} %reduce-scatter.8.cloned.1.call-done, f32[3584]{0:T(1024)S(1)} %add_convert_fusion), kind=kLoop, calls=%fused_computation.3 | loop fusion | flops 7340032 | bytes 22034432 | tf_op jit(solution)/shard_map/mul | solution.py:20
  424.4 23.1 %convolution_multiply_fusion = f32[1024,28,128]{0,2,1:T(8,128)} fusion(f32[1024,28,128]{0,2,1:T(8,128)} %bitcast.27), kind=kOutput, calls=%fused_computation.5 | convolution fusion | flops 5641388032 | bytes 29360128 | tf_op jit(solution)/shard_map/rbi,ij->rbj/dot_general | solution.py:22
  447.5 14.3 %copy.31 = f32[1024,3584]{1,0:T(8,128)} copy(f32[1024,3584]{0,1:T(8,128)} %bitcast.26) | data formatting | bytes 29360128
  (20 shorter events, 0.5 us)
Async XLA Ops:
  7.2 10.5 %copy-start.2 = (f32[16,3584]{1,0:T(8,128)S(1)}, f32[16,3584]{1,0:T(8,128)}, u32[]{:S(2)}) copy-start(f32[16,3584]{1,0:T(8,128)} %param.7) | copy-start | bytes 688132
  11.3 54.5 %all-to-all-start = ((bf16[128,4,2048]{0,2,1:T(8,128)(2,1)}), bf16[128,4,2048]{0,2,1:T(8,128)(2,1)S(1)}, u32[]{:S(2)}, u32[]{:S(2)}) async-start(bf16[128,4,2048]{0,2,1:T(8,128)(2,1)} %bitcast.30), calls=%async_computation | async-start | bytes 4194304 | tf_op jit(solution)/shard_map/all_to_all | solution.py:38
  17.6 137.8 %reduce-scatter.10.cloned.1.call-start = ((), (), s32[]{:S(2)}) async-start(), calls=%async_computation.7 | async-start | bytes 4587520
  81.6 6.2 %copy-start.1 = (bf16[128,3584]{1,0:T(8,128)(2,1)S(1)}, bf16[128,3584]{1,0:T(8,128)(2,1)}, u32[]{:S(2)}) copy-start(bf16[128,3584]{1,0:T(8,128)(2,1)} %param.8) | copy-start | bytes 2752516
  87.7 327.1 %reduce-scatter.8.cloned.1.call-start = ((), (), s32[]{:S(2)}) async-start(), calls=%async_computation.6 | async-start | bytes 22020096 | tf_op jit(solution)/shard_map/reduce_scatter | solution.py:73
  159.7 23.6 %collective-permute-start = (bf16[128,3584]{0,1:T(8,128)(2,1)S(1)}, bf16[128,3584]{0,1:T(8,128)(2,1)S(1)}, u32[]{:S(2)}, u32[]{:S(2)}) collective-permute-start(bf16[128,3584]{0,1:T(8,128)(2,1)S(1)} %get-tuple-element.15), channel_id=1, source_target_pairs={{0,8},{8,16},{16,24},{24,0},{1,9},{9,17},{17,25},{25,1},{2,10},{10... | collective-permute-start | bytes 2752520 | tf_op jit(solution)/shard_map/ppermute | solution.py:53
  183.3 22.8 %collective-permute-start.1 = (bf16[128,3584]{0,1:T(8,128)(2,1)S(1)}, bf16[128,3584]{0,1:T(8,128)(2,1)}, u32[]{:S(2)}, u32[]{:S(2)}) collective-permute-start(bf16[128,3584]{0,1:T(8,128)(2,1)S(1)} %collective-permute-done), channel_id=1, source_target_pairs={{0,8},{8,16},{16,24},{24,0},{1,9},{9,17},{17,25},{25,1},{2,10},{10... | collective-permute-start | bytes 2752520 | tf_op jit(solution)/shard_map/ppermute | solution.py:53
  206.1 22.1 %collective-permute-start.2 = (bf16[128,3584]{0,1:T(8,128)(2,1)}, bf16[128,3584]{0,1:T(8,128)(2,1)}, u32[]{:S(2)}, u32[]{:S(2)}) collective-permute-start(bf16[128,3584]{0,1:T(8,128)(2,1)} %collective-permute-done.1), channel_id=1, source_target_pairs={{0,8},{8,16},{16,24},{24,0},{1,9},{9,17},{17,25},{25,1},{2,10},{10... | collective-permute-start | bytes 2752520 | tf_op jit(solution)/shard_map/ppermute | solution.py:53
  206.1 32.3 %copy-start = (bf16[4,128,2048]{2,1,0:T(8,128)(2,1)S(1)}, bf16[4,128,2048]{2,1,0:T(8,128)(2,1)}, u32[]{:S(2)}) copy-start(bf16[4,128,2048]{2,1,0:T(8,128)(2,1)} %copy.26) | copy-start | bytes 6291460
  235.4 3.0 copy-start.3
  249.4 212.3 %reduce-scatter.6.cloned.1.call-start = ((), (), s32[]{:S(2)}) async-start(), calls=%async_computation.5 | async-start | bytes 2621440 | tf_op jit(solution)/shard_map/reduce_scatter | solution.py:67
  261.8 49.5 %copy-start.4 = (s32[3584]{0:T(1024)S(1)}, s32[3584]{0:T(1024)}, u32[]{:S(2)}) copy-start(s32[3584]{0:T(1024)} %param.9) | copy-start | bytes 43012
Sparse Core Ops, SparseCore 0:
  87.8 67.6 reduce-scatter.9
  249.6 165.2 reduce-scatter.7
  417.9 31.1 reduce-scatter.5
